TPU v7x, 32 devices: a whole 2x2x4 slice. The times are simulated.
32 devices in a mesh: dp: 4 (over z), expert: 8 (over y, x, core).
Axes of the slice: x: 2, y: 2, z: 4, core: 2. Of those that a mesh axis runs over, the one named last changes fastest.
Arguments:
- tokens: bfloat16 [8192, 1280], P(('dp', 'expert')), may hold values from -14 to 14
- ln_gain: float32 [1280], replicated, may hold values from 0.25 to 1.75
- router: bfloat16 [1280, 8], replicated, may hold values from -0.3125 to 0.3125
- w_in: bfloat16 [8, 5120, 1280], P('expert', 'dp'), may hold values from -0.15625 to 0.15625
- b_in: bfloat16 [8, 5120], P('expert', 'dp'), may hold values from -3 to 3
- w_out: bfloat16 [8, 5120, 1280], P('expert', 'dp'), may hold values from -0.078125 to 0.078125
- b_out: bfloat16 [8, 1280], P('expert'), may hold values from -3 to 3
- expert_choice: int32 [8192], P(('dp', 'expert')), may hold values from 0 to 7
- modality: int32 [8192], P(('dp', 'expert')), may hold values from 0 to 1, as said below
- slot: int32 [8192], P(('dp', 'expert')), may hold values from -1 to 15, as said below
Outputs:
- moe_out: bfloat16 [8192, 1280], P(('dp', 'expert'))
- aux_losses: float32 [2, 2], replicated
Inputs may be any that keep to these rules, and one draw needn't show every extreme that they name: Each source's tokens with one expert and a slot other than -1 have distinct slots, numbered from 0 in token order; one expert has all 16 slots filled in every source. `modality`: every source holds tokens of both modalities.
All inputs are finite; a program needn't handle non-finite values.
Results may differ from a plain program's by a relative error of at most 0.007.
Values may be sent and summed in bfloat16 or wider, within the bound.
No kernel may reach another device: no remote copies, remote signals or barrier semaphores. Data moves between devices by JAX's collectives and lax.ppermute only.
A program may use at most 128 MiB of HBM per device.

v0:
```python
import jax
import jax.numpy as jnp
from jax import lax
from jax.sharding import PartitionSpec as P

CAP = 16


def layer_norm(tokens, ln_gain):
    values = tokens.astype(jnp.float32)
    center = values - jnp.mean(values, axis=-1, keepdims=True)
    spread = jnp.mean(center * center, axis=-1, keepdims=True)
    return (center * lax.rsqrt(spread + 1e-06) * ln_gain).astype(jnp.bfloat16)


def expert_hidden(rows, first, first_bias, second):
    pre = lax.dot_general(rows, first, (((1,), (1,)), ((), ())), preferred_element_type=jnp.float32)
    hidden = jax.nn.gelu(pre + first_bias.astype(jnp.float32), approximate=False).astype(
        jnp.bfloat16
    )
    return jnp.dot(hidden, second, preferred_element_type=jnp.float32)


def on_device(tokens, ln_gain, router, w_in, b_in, w_out, b_out, expert_choice, modality, slot):
    normed = layer_norm(tokens, ln_gain)
    logits = jnp.dot(normed, router, preferred_element_type=jnp.float32)
    logp = jax.nn.log_softmax(logits, axis=-1)
    probs = jnp.exp(logp)
    gate = jnp.take_along_axis(probs, expert_choice[:, None], axis=1)[:, 0]
    experts_all = router.shape[1]
    width = normed.shape[1]
    columns = experts_all * CAP
    target = jnp.where(slot >= 0, expert_choice * CAP + slot, -1)
    table = (target[:, None] == jnp.arange(columns, dtype=jnp.int32)[None, :]).astype(jnp.bfloat16)
    buffer = jnp.einsum("tk,td->kd", table, normed, preferred_element_type=jnp.float32).astype(
        jnp.bfloat16
    )
    received = lax.all_to_all(
        buffer.reshape(experts_all, CAP, width), "expert", split_axis=0, concat_axis=0, tiled=True
    )
    senders = lax.axis_size("expert")
    local_count = w_in.shape[0]
    received = received.reshape(senders, local_count, CAP, width)
    rows = received[:, 0].reshape(senders * CAP, width)
    gathered = lax.all_gather(rows, "dp", axis=0, tiled=True)
    summed = lax.psum_scatter(
        expert_hidden(gathered, w_in[0], b_in[0], w_out[0]), "dp", scatter_dimension=0, tiled=True
    )
    results = [
        (summed + b_out[0].astype(jnp.float32)).astype(jnp.bfloat16).reshape(senders, CAP, width)
    ]
    outputs = jnp.stack(results, axis=1).reshape(experts_all, CAP, width)
    returned = lax.all_to_all(outputs, "expert", split_axis=0, concat_axis=0, tiled=True)
    fetched = jnp.dot(table, returned.reshape(columns, width), preferred_element_type=jnp.float32)
    moe_out = (gate[:, None] * fetched).astype(jnp.bfloat16)
    textual = (modality == 1).astype(jnp.float32)
    select = jnp.stack([1.0 - textual, textual], axis=0)
    entropy = -jnp.sum(probs * logp, axis=-1)
    prob_part = jnp.dot(select, probs, precision=lax.Precision.HIGHEST)
    ent_part = jnp.dot(select, entropy, precision=lax.Precision.HIGHEST)
    count_part = jnp.sum(select, axis=1)
    prob_sum, ent_sum, count = lax.psum((prob_part, ent_part, count_part), ("dp", "expert"))
    pbar = prob_sum / count[:, None]
    aux_losses = jnp.stack([ent_sum / count, jnp.sum(pbar * jnp.log(pbar), axis=1)], axis=1)
    return (moe_out, aux_losses)


def solution(mesh):
    return jax.shard_map(
        on_device,
        mesh=mesh,
        in_specs=(
            P(("dp", "expert"), None),
            P(),
            P(),
            P("expert", "dp", None),
            P("expert", "dp"),
            P("expert", "dp", None),
            P("expert", None),
            P(("dp", "expert")),
            P(("dp", "expert")),
            P(("dp", "expert")),
        ),
        out_specs=(P(("dp", "expert"), None), P()),
        check_vma=False,
    )
```

profile of v0, /device:TPU:0, one launch (start us, length us, event | category | flops | bytes accessed | tf_op | source)
XLA Modules:
  0.0 144.7 jit_solution(16310733744528008156)
XLA Ops:
  7.2 0.0 copy-start
  7.2 0.0 copy-start.6
  7.2 0.0 copy-start.7
  7.2 0.0 copy-start.3
  7.2 0.0 all-gather.2.cloned.1.call-start
  7.3 1.4 convert_reduce_fusion
  8.7 1.4 fusion.18
  10.1 1.4 fusion.20
  11.4 0.0 copy-done.6
  11.5 0.0 copy-done.7
  11.5 0.0 copy-start.1
  11.5 0.8 copy-done.1
  12.3 0.4 convolution_convert_fusion
  12.7 12.7 %all_to_all.10 = bf16[8,16,1280]{2,1,0:T(8,128)(2,1)} all-to-all(bf16[8,16,1280]{2,1,0:T(8,128)(2,1)S(1)} %bitcast.35), channel_id=1, replica_groups=mesh['dp'=4,'expert'=8] {'expert'}, dimensions={0} | all-to-all | bytes 655360 | tf_op jit(solution)/shard_map/all_to_all | solution.py:38
  25.4 0.0 all-gather.2.cloned.1.call-update
  25.4 0.0 reduce-scatter.2.cloned.1.call-start
  25.5 0.0 copy-done.3
  25.5 32.0 %all-gather.2.cloned.1.call-done = bf16[512,1280]{1,0:T(8,128)(2,1)} async-done(((bf16[128,1280]{1,0:T(8,128)(2,1)}), bf16[512,1280]{1,0:T(8,128)(2,1)}) %all-gather.2.cloned.1.call-update) | async-done | bytes 1310736 | tf_op jit(solution)/shard_map/all_gather | solution.py:45
  57.4 0.0 copy-done
  57.5 12.3 %fusion = f32[512,1280]{1,0:T(8,128)} fusion(bf16[1,1280,1280]{2,1,0:T(8,128)(2,1)S(1)} %copy-done, bf16[512,1280]{1,0:T(8,128)(2,1)} %all-gather.2.cloned.1.call-done, bf16[1,1280,1280]{2,1,0:T(8,128)(2,1)} %param.13, f32[1280]{0:T(1024)S(1)} %convert_reduce_fusion.2), kind=kOutput, calls=%fused_computation.3 | convolution fusion | flops 3398696960 | bytes 10490880 | tf_op jit(solution)/shard_map/dot_general | solution.py:21
  69.8 0.0 copy-start.2
  69.8 0.0 copy-start.5
  69.8 0.0 copy-start.4
  69.8 0.0 reduce-scatter.2.cloned.1.call-update
  69.8 0.7 copy-done.2
  70.5 1.4 fusion.61
  72.0 0.0 copy-done.5
  72.0 0.1 convolution_bitcast_fusion
  72.1 0.1 fusion.29
  72.3 0.1 fusion.60
  72.4 41.3 %all-reduce = (f32[2,8]{1,0:T(2,128)S(1)}, f32[2]{0:T(128)S(1)}, f32[2]{0:T(128)S(1)}) all-reduce(f32[2,8]{1,0:T(2,128)S(1)} %fusion.29, f32[2]{0:T(128)S(1)} %fusion.60, f32[2]{0:T(128)S(1)} %convolution_bitcast_fusion), channel_id=1, replica_groups=mesh['dp'=4,'expert'=8] {'dp','expert'}, use_global_device_ids=true, to_apply=%region_9.10 | all-reduce | flops 20 | bytes 160 | tf_op jit(solution)/shard_map/psum | solution.py:62
  113.7 0.0 copy-done.4
  113.7 0.2 fusion.25
  114.0 8.2 %reduce-scatter.2.cloned.1.call-done = f32[128,1280]{1,0:T(8,128)} async-done(((f32[512,1280]{1,0:T(8,128)}), f32[128,1280]{1,0:T(8,128)}) %reduce-scatter.2.cloned.1.call-update) | async-done | bytes 655376 | tf_op jit(solution)/shard_map/reduce_scatter | solution.py:46
  122.1 1.9 %add_convert_fusion = bf16[128,1280]{1,0:T(8,128)(2,1)} fusion(f32[128,1280]{1,0:T(8,128)} %reduce-scatter.2.cloned.1.call-done, f32[1280]{0:T(1024)S(1)} %convert_reduce_fusion.1), kind=kLoop, calls=%fused_computation.35 | loop fusion | flops 327680 | bytes 988160 | tf_op jit(solution)/shard_map/convert_element_type | solution.py:50
  124.0 4.1 %all-to-all-start.1 = ((bf16[8,16,1280]{2,1,0:T(8,128)(2,1)}), bf16[8,16,1280]{2,1,0:T(8,128)(2,1)}, u32[]{:S(2)}, u32[]{:S(2)}) async-start(bf16[8,16,1280]{2,1,0:T(8,128)(2,1)} %bitcast.33), calls=%async_computation.2 | async-start | bytes 655360 | tf_op jit(solution)/shard_map/all_to_all | solution.py:53
  128.1 0.6 copy.14
  128.7 1.8 %gather_fusion = f32[256]{0:T(256)S(1)} fusion(f32[256,8]{0,1:T(8,128)S(1)} %get-tuple-element.12, s32[256]{0:T(256)S(1)} %bitcast.32), kind=kCustom, calls=%fused_computation | custom fusion | bytes 4096 | tf_op jit(solution)/shard_map/jit(take_along_axis)/gather | solution.py:29
  130.6 5.1 %all-to-all-done.1 = bf16[8,16,1280]{2,1,0:T(8,128)(2,1)} async-done(((bf16[8,16,1280]{2,1,0:T(8,128)(2,1)}), bf16[8,16,1280]{2,1,0:T(8,128)(2,1)}, u32[]{:S(2)}, u32[]{:S(2)}) %all-to-all-start.1) | async-done | bytes 327712 | tf_op jit(solution)/shard_map/all_to_all | solution.py:53
  135.7 2.2 %fusion.15 = bf16[256,1280]{1,0:T(8,128)(2,1)} fusion(bf16[128,1280]{1,0:T(8,128)(2,1)} %bitcast.8, f32[256]{0:T(256)S(1)} %and_select_fusion, s32[256]{0:T(256)S(1)} %get-tuple-element.14), kind=kOutput, calls=%fused_computation.25 | convolution fusion | flops 84574208 | bytes 985088 | tf_op jit(solution)/shard_map/dot_general | solution.py:54
  (17 shorter events, 0.2 us)
Async XLA Ops:
  7.2 50.3 %copy-start = (bf16[1,1280,1280]{2,1,0:T(8,128)(2,1)S(1)}, bf16[1,1280,1280]{2,1,0:T(8,128)(2,1)}, u32[]{:S(2)}) copy-start(bf16[1,1280,1280]{2,1,0:T(8,128)(2,1)} %param.15) | copy-start | bytes 9830404
  7.2 4.3 %copy-start.6 = (s32[256]{0:T(256)S(1)}, s32[256]{0:T(256)}, u32[]{:S(2)}) copy-start(s32[256]{0:T(256)} %param.17) | copy-start | bytes 3076
  7.2 4.3 %copy-start.7 = (s32[256]{0:T(256)S(1)}, s32[256]{0:T(256)}, u32[]{:S(2)}) copy-start(s32[256]{0:T(256)} %param.19) | copy-start | bytes 3076
  7.2 18.3 %copy-start.3 = (bf16[1,1280]{1,0:T(2,128)(2,1)S(1)}, bf16[1,1280]{1,0:T(2,128)(2,1)}, u32[]{:S(2)}) copy-start(bf16[1,1280]{1,0:T(2,128)(2,1)} %param.14) | copy-start | bytes 7684
  7.2 50.2 %all-gather.2.cloned.1.call-start = ((), (), s32[]{:S(2)}) async-start(), calls=%async_computation.3 | async-start | bytes 1638400 | tf_op jit(solution)/shard_map/all_gather | solution.py:45
  11.5 0.8 copy-start.1
  25.4 96.7 %reduce-scatter.2.cloned.1.call-start = ((), (), s32[]{:S(2)}) async-start(), calls=%async_computation.4 | async-start | bytes 3276800 | tf_op jit(solution)/shard_map/reduce_scatter | solution.py:46
  69.8 0.7 copy-start.2
  69.8 2.2 %copy-start.5 = (s32[256]{0:T(256)S(1)}, s32[256]{0:T(256)}, u32[]{:S(2)}) copy-start(s32[256]{0:T(256)} %param.18) | copy-start | bytes 3076
  69.8 44.0 %copy-start.4 = (bf16[1,1280]{1,0:T(2,128)(2,1)S(1)}, bf16[1,1280]{1,0:T(2,128)(2,1)}, u32[]{:S(2)}) copy-start(bf16[1,1280]{1,0:T(2,128)(2,1)} %param.16) | copy-start | bytes 7684
  124.0 11.7 %all-to-all-start.1 = ((bf16[8,16,1280]{2,1,0:T(8,128)(2,1)}), bf16[8,16,1280]{2,1,0:T(8,128)(2,1)}, u32[]{:S(2)}, u32[]{:S(2)}) async-start(bf16[8,16,1280]{2,1,0:T(8,128)(2,1)} %bitcast.33), calls=%async_computation.2 | async-start | bytes 655360 | tf_op jit(solution)/shard_map/all_to_all | solution.py:53
Sparse Core Ops, SparseCore 0:
  25.5 31.8 all-gather.1
  69.9 52.1 reduce-scatter.1
where the time goes:
time: 145 us
  blocking collectives  54 us (37%)
  waiting for transfers between devices  45.3 us (31%)
  matrix products  16.5 us (11%)
  between operations  14.3 us (10%)
  other arithmetic  6.49 us (4%)
  starting transfers between devices  4.15 us (3%)
  local copies, waits for them, and re-layouts  4.02 us (3%)
    psum x1, blocking collectives, on_device(): lax.psum((prob_part, ent_part, count_part), ('dp', 'expert'))  41.3 us
    all_gather x1, waiting for transfers between devices, on_device(): gathered = lax.all_gather(rows, 'dp', axis=0, tiled=True)  32 us
    all_to_all x1, blocking collectives, on_device(): lax.all_to_all(buffer.reshape(experts_all, CAP, width), 'expert', split_a...  12.7 us
    dot_general x1, matrix products, expert_hidden(): return jnp.dot(hidden, second, preferred_element_type=jnp.float32)  12.3 us
    reduce_scatter x1, waiting for transfers between devices, on_device(): lax.psum_scatter(expert_hidden(gathered, w_in[0], b_in[0], w_out[0]), 'dp...  8.17 us
    all_to_all x1, waiting for transfers between devices, on_device(): lax.all_to_all(outputs, 'expert', split_axis=0, concat_axis=0, tiled=True)  5.12 us
    all_to_all x1, starting transfers between devices, on_device(): lax.all_to_all(outputs, 'expert', split_axis=0, concat_axis=0, tiled=True)  4.07 us
  transfers between devices with their start and end apart: 3, of which 3 were waited for; matrix products, arithmetic and copies ran while one was open for 3% of the time, Pallas kernels for 0%

commit v1 on v0

--- a/solution.py
+++ b/solution.py
@@ -59,7 +59,7 @@
     prob_part = jnp.dot(select, probs, precision=lax.Precision.HIGHEST)
     ent_part = jnp.dot(select, entropy, precision=lax.Precision.HIGHEST)
     count_part = jnp.sum(select, axis=1)
-    prob_sum, ent_sum, count = lax.psum((prob_part, ent_part, count_part), ("dp", "expert"))
+    prob_sum, ent_sum, count = lax.psum(lax.psum((prob_part, ent_part, count_part), "expert"), "dp")
     pbar = prob_sum / count[:, None]
     aux_losses = jnp.stack([ent_sum / count, jnp.sum(pbar * jnp.log(pbar), axis=1)], axis=1)
     return (moe_out, aux_losses)

time: 145 us -> 145 us (level)
  blocking collectives: 54 us -> 36.9 us
  waiting for transfers between devices: 45.3 us -> 61.7 us
    psum x1 -> x2, blocking collectives: 41.3 us -> 24.2 us  [the longest x1 12.9 us: on_device(): lax.psum((prob_part, ent_part, count_part), 'expert')]
    reduce_scatter x1, waiting for transfers between devices: 8.17 us -> 24.6 us  [on_device(): lax.psum_scatter(expert_hidden(gathered, w_in[0], b_in[0], w_out[0]), 'dp...]
where the time goes in v1:
time: 145 us; the launch traced here: 144 us
  waiting for transfers between devices  61.7 us (43%)
  blocking collectives  36.9 us (25%)
  matrix products  16.5 us (11%)
  between operations  14.3 us (10%)
  other arithmetic  6.49 us (4%)
  starting transfers between devices  4.15 us (3%)
  local copies, waits for them, and re-layouts  4.02 us (3%)
    all_gather x1, waiting for transfers between devices, on_device(): gathered = lax.all_gather(rows, 'dp', axis=0, tiled=True)  32 us
    reduce_scatter x1, waiting for transfers between devices, on_device(): lax.psum_scatter(expert_hidden(gathered, w_in[0], b_in[0], w_out[0]), 'dp...  24.6 us
    psum x1, blocking collectives, on_device(): lax.psum((prob_part, ent_part, count_part), 'expert')  12.9 us
    all_to_all x1, blocking collectives, on_device(): lax.all_to_all(buffer.reshape(experts_all, CAP, width), 'expert', split_a...  12.7 us
    dot_general x1, matrix products, expert_hidden(): return jnp.dot(hidden, second, preferred_element_type=jnp.float32)  12.3 us
    psum x1, blocking collectives, on_device(): lax.psum(lax.psum((prob_part, ent_part, count_part), 'expert'), 'dp')  11.3 us
    all_to_all x1, waiting for transfers between devices, on_device(): lax.all_to_all(outputs, 'expert', split_axis=0, concat_axis=0, tiled=True)  5.12 us
    all_to_all x1, starting transfers between devices, on_device(): lax.all_to_all(outputs, 'expert', split_axis=0, concat_axis=0, tiled=True)  4.07 us
  transfers between devices with their start and end apart: 3, of which 3 were waited for; matrix products, arithmetic and copies ran while one was open for 3% of the time, Pallas kernels for 0%

profile of v1, /device:TPU:0, one launch (start us, length us, event | category | flops | bytes accessed | tf_op | source)
XLA Modules:
  0.0 144.1 jit_solution(17298223870674617863)
XLA Ops:
  7.2 0.0 copy-start
  7.2 0.0 copy-start.6
  7.2 0.0 copy-start.7
  7.2 0.0 copy-start.3
  7.2 0.0 all-gather.2.cloned.1.call-start
  7.3 1.4 convert_reduce_fusion
  8.7 1.4 fusion.18
  10.1 1.4 fusion.20
  11.4 0.0 copy-done.6
  11.5 0.0 copy-done.7
  11.5 0.0 copy-start.1
  11.5 0.8 copy-done.1
  12.3 0.4 convolution_convert_fusion
  12.7 12.7 %all_to_all.10 = bf16[8,16,1280]{2,1,0:T(8,128)(2,1)} all-to-all(bf16[8,16,1280]{2,1,0:T(8,128)(2,1)S(1)} %bitcast.35), channel_id=1, replica_groups=mesh['dp'=4,'expert'=8] {'expert'}, dimensions={0} | all-to-all | bytes 655360 | tf_op jit(solution)/shard_map/all_to_all | solution.py:38
  25.4 0.0 all-gather.2.cloned.1.call-update
  25.4 0.0 reduce-scatter.2.cloned.1.call-start
  25.5 0.0 copy-done.3
  25.5 32.0 %all-gather.2.cloned.1.call-done = bf16[512,1280]{1,0:T(8,128)(2,1)} async-done(((bf16[128,1280]{1,0:T(8,128)(2,1)}), bf16[512,1280]{1,0:T(8,128)(2,1)}) %all-gather.2.cloned.1.call-update) | async-done | bytes 1310736 | tf_op jit(solution)/shard_map/all_gather | solution.py:45
  57.4 0.0 copy-done
  57.5 12.3 %fusion = f32[512,1280]{1,0:T(8,128)} fusion(bf16[1,1280,1280]{2,1,0:T(8,128)(2,1)S(1)} %copy-done, bf16[512,1280]{1,0:T(8,128)(2,1)} %all-gather.2.cloned.1.call-done, bf16[1,1280,1280]{2,1,0:T(8,128)(2,1)} %param.13, f32[1280]{0:T(1024)S(1)} %convert_reduce_fusion.2), kind=kOutput, calls=%fused_computation.3 | convolution fusion | flops 3398696960 | bytes 10490880 | tf_op jit(solution)/shard_map/dot_general | solution.py:21
  69.8 0.0 copy-start.2
  69.8 0.0 copy-start.5
  69.8 0.0 copy-start.4
  69.8 0.0 reduce-scatter.2.cloned.1.call-update
  69.8 0.7 copy-done.2
  70.5 1.4 fusion.61
  72.0 0.0 copy-done.5
  72.0 0.1 convolution_bitcast_fusion
  72.1 0.1 fusion.29
  72.3 0.1 fusion.60
  72.4 12.9 %all-reduce = (f32[2,8]{1,0:T(2,128)S(1)}, f32[2]{0:T(128)S(1)}, f32[2]{0:T(128)S(1)}) all-reduce(f32[2,8]{1,0:T(2,128)S(1)} %fusion.29, f32[2]{0:T(128)S(1)} %fusion.60, f32[2]{0:T(128)S(1)} %convolution_bitcast_fusion), channel_id=1, replica_groups=mesh['dp'=4,'expert'=8] {'expert'}, use_global_device_ids=true, to_apply=%region_11.12 | all-reduce | flops 20 | bytes 160 | tf_op jit(solution)/shard_map/psum | solution.py:62
  85.4 11.3 %all-reduce.1 = (f32[2,8]{1,0:T(2,128)S(1)}, f32[2]{0:T(128)S(1)}, f32[2]{0:T(128)S(1)}) all-reduce(f32[2,8]{1,0:T(2,128)S(1)} %get-tuple-element.8, f32[2]{0:T(128)S(1)} %get-tuple-element.9, f32[2]{0:T(128)S(1)} %get-tuple-element.10), channel_id=1, replica_groups=mesh['dp'=4,'expert'=8] {'dp'}, use_global_device_ids=true, to_apply=%region_12.13 | all-reduce | flops 20 | bytes 160 | tf_op jit(solution)/shard_map/psum | solution.py:62
  96.7 0.0 copy-done.4
  96.7 0.2 fusion.25
  96.9 24.6 %reduce-scatter.2.cloned.1.call-done = f32[128,1280]{1,0:T(8,128)} async-done(((f32[512,1280]{1,0:T(8,128)}), f32[128,1280]{1,0:T(8,128)}) %reduce-scatter.2.cloned.1.call-update) | async-done | bytes 655376 | tf_op jit(solution)/shard_map/reduce_scatter | solution.py:46
  121.5 1.9 %add_convert_fusion = bf16[128,1280]{1,0:T(8,128)(2,1)} fusion(f32[128,1280]{1,0:T(8,128)} %reduce-scatter.2.cloned.1.call-done, f32[1280]{0:T(1024)S(1)} %convert_reduce_fusion.1), kind=kLoop, calls=%fused_computation.35 | loop fusion | flops 327680 | bytes 988160 | tf_op jit(solution)/shard_map/convert_element_type | solution.py:50
  123.3 4.1 %all-to-all-start.1 = ((bf16[8,16,1280]{2,1,0:T(8,128)(2,1)}), bf16[8,16,1280]{2,1,0:T(8,128)(2,1)}, u32[]{:S(2)}, u32[]{:S(2)}) async-start(bf16[8,16,1280]{2,1,0:T(8,128)(2,1)} %bitcast.33), calls=%async_computation.2 | async-start | bytes 655360 | tf_op jit(solution)/shard_map/all_to_all | solution.py:53
  127.4 0.6 copy.14
  128.1 1.8 %gather_fusion = f32[256]{0:T(256)S(1)} fusion(f32[256,8]{0,1:T(8,128)S(1)} %get-tuple-element.15, s32[256]{0:T(256)S(1)} %bitcast.32), kind=kCustom, calls=%fused_computation | custom fusion | bytes 4096 | tf_op jit(solution)/shard_map/jit(take_along_axis)/gather | solution.py:29
  129.9 5.1 %all-to-all-done.1 = bf16[8,16,1280]{2,1,0:T(8,128)(2,1)} async-done(((bf16[8,16,1280]{2,1,0:T(8,128)(2,1)}), bf16[8,16,1280]{2,1,0:T(8,128)(2,1)}, u32[]{:S(2)}, u32[]{:S(2)}) %all-to-all-start.1) | async-done | bytes 327712 | tf_op jit(solution)/shard_map/all_to_all | solution.py:53
  135.0 2.2 %fusion.15 = bf16[256,1280]{1,0:T(8,128)(2,1)} fusion(bf16[128,1280]{1,0:T(8,128)(2,1)} %bitcast.8, f32[256]{0:T(256)S(1)} %and_select_fusion, s32[256]{0:T(256)S(1)} %get-tuple-element.17), kind=kOutput, calls=%fused_computation.25 | convolution fusion | flops 84574208 | bytes 985088 | tf_op jit(solution)/shard_map/dot_general | solution.py:54
  (17 shorter events, 0.2 us)
Async XLA Ops:
  7.2 50.3 %copy-start = (bf16[1,1280,1280]{2,1,0:T(8,128)(2,1)S(1)}, bf16[1,1280,1280]{2,1,0:T(8,128)(2,1)}, u32[]{:S(2)}) copy-start(bf16[1,1280,1280]{2,1,0:T(8,128)(2,1)} %param.15) | copy-start | bytes 9830404
  7.2 4.3 %copy-start.6 = (s32[256]{0:T(256)S(1)}, s32[256]{0:T(256)}, u32[]{:S(2)}) copy-start(s32[256]{0:T(256)} %param.17) | copy-start | bytes 3076
  7.2 4.3 %copy-start.7 = (s32[256]{0:T(256)S(1)}, s32[256]{0:T(256)}, u32[]{:S(2)}) copy-start(s32[256]{0:T(256)} %param.19) | copy-start | bytes 3076
  7.2 18.3 %copy-start.3 = (bf16[1,1280]{1,0:T(2,128)(2,1)S(1)}, bf16[1,1280]{1,0:T(2,128)(2,1)}, u32[]{:S(2)}) copy-start(bf16[1,1280]{1,0:T(2,128)(2,1)} %param.14) | copy-start | bytes 7684
  7.2 50.2 %all-gather.2.cloned.1.call-start = ((), (), s32[]{:S(2)}) async-start(), calls=%async_computation.3 | async-start | bytes 1638400 | tf_op jit(solution)/shard_map/all_gather | solution.py:45
  11.5 0.8 copy-start.1
  25.4 96.1 %reduce-scatter.2.cloned.1.call-start = ((), (), s32[]{:S(2)}) async-start(), calls=%async_computation.4 | async-start | bytes 3276800 | tf_op jit(solution)/shard_map/reduce_scatter | solution.py:46
  69.8 0.7 copy-start.2
  69.8 2.2 %copy-start.5 = (s32[256]{0:T(256)S(1)}, s32[256]{0:T(256)}, u32[]{:S(2)}) copy-start(s32[256]{0:T(256)} %param.18) | copy-start | bytes 3076
  69.8 26.9 %copy-start.4 = (bf16[1,1280]{1,0:T(2,128)(2,1)S(1)}, bf16[1,1280]{1,0:T(2,128)(2,1)}, u32[]{:S(2)}) copy-start(bf16[1,1280]{1,0:T(2,128)(2,1)} %param.16) | copy-start | bytes 7684
  123.3 11.7 %all-to-all-start.1 = ((bf16[8,16,1280]{2,1,0:T(8,128)(2,1)}), bf16[8,16,1280]{2,1,0:T(8,128)(2,1)}, u32[]{:S(2)}, u32[]{:S(2)}) async-start(bf16[8,16,1280]{2,1,0:T(8,128)(2,1)} %bitcast.33), calls=%async_computation.2 | async-start | bytes 655360 | tf_op jit(solution)/shard_map/all_to_all | solution.py:53
Sparse Core Ops, SparseCore 0:
  25.5 31.8 all-gather.1
  69.9 51.5 reduce-scatter.1
